TPU v7x, 32 devices: a whole 2x2x4 slice. The times are simulated.
32 devices in a mesh: dp: 8 (over z, y), tensor: 4 (over x, core).
Axes of the slice: x: 2, y: 2, z: 4, core: 2. Of those that a mesh axis runs over, the one named last changes fastest.
Arguments:
- tokens: bfloat16 [16384, 768], P('dp'), may hold values from -6 to 6
- w_query: bfloat16 [768, 768], P(None, 'tensor'), may hold values from -0.21875 to 0.21875
- w_key: bfloat16 [768, 768], P(None, 'tensor'), may hold values from -0.21875 to 0.21875
- w_value: bfloat16 [768, 768], P(None, 'tensor'), may hold values from -0.21875 to 0.21875
- b_query: float32 [768], P('tensor'), may hold values from -4 to 4
- b_value: float32 [768], P('tensor'), may hold values from -3 to 3
- conv_taps: float32 [12, 33], P('tensor'), may hold values from -0.3 to 0.3
- w_out: bfloat16 [768, 768], P('tensor'), may hold values from -0.875 to 0.875
- b_out: float32 [768], replicated, may hold values from -3 to 3
- gain_one: float32 [768], replicated, may hold values from 0.5 to 1.5
- shift_one: float32 [768], replicated, may hold values from -3 to 3
- w_up: bfloat16 [768, 3072], P(None, 'tensor'), may hold values from -0.21875 to 0.21875
- b_up: float32 [3072], P('tensor'), may hold values from -3 to 3
- w_down: bfloat16 [3072, 768], P('tensor'), may hold values from -0.109375 to 0.109375
- b_down: float32 [768], replicated, may hold values from -3 to 3
- gain_two: float32 [768], replicated, may hold values from 0.5 to 1.5
- shift_two: float32 [768], replicated, may hold values from -3 to 3
- cotangent: bfloat16 [16384, 768], P(('dp', 'tensor')), may hold values from -6 to 6
- segment_ids: int32 [16384], P('dp'), may hold values from 0 to 7, as said below
- landmark_ids: int32 [16384], P('dp'), may hold values from 0 to 63, as said below
Outputs:
- layer_out: bfloat16 [16384, 768], P(('dp', 'tensor'))
- input_grad: float32 [16384, 768], P(('dp', 'tensor'))
- grad_w_query: float32 [768, 768], P(None, 'tensor')
- grad_w_key: float32 [768, 768], P(None, 'tensor')
- grad_w_value: float32 [768, 768], P(None, 'tensor')
- grad_b_query: float32 [768], P('tensor')
- grad_b_value: float32 [768], P('tensor')
- grad_conv: float32 [12, 33], P('tensor')
- grad_w_out: float32 [768, 768], P('tensor')
- grad_b_out: float32 [768], replicated
- grad_gain_one: float32 [768], replicated
- grad_shift_one: float32 [768], replicated
- grad_w_up: float32 [768, 3072], P(None, 'tensor')
- grad_b_up: float32 [3072], P('tensor')
- grad_w_down: float32 [3072, 768], P('tensor')
- grad_b_down: float32 [768], replicated
- grad_gain_two: float32 [768], replicated
- grad_shift_two: float32 [768], replicated
Inputs may be any that keep to these rules, and one draw needn't show every extreme that they name: `segment_ids`: within each sequence of 1024 tokens the ids never fall and take every value from 0 to 7; every document holds 64 tokens or more. `landmark_ids`: within each sequence every id from 0 to 63 occurs, and the tokens with id j form one run inside document j // 8.
All inputs are finite; a program needn't handle non-finite values.
Results may differ from a plain program's by a relative error of at most 0.015.
Values may be sent and summed in bfloat16 or wider, within the bound.
No kernel may reach another device: no remote copies, remote signals or barrier semaphores. Data moves between devices by JAX's collectives and lax.ppermute only.
A program may use at most 256 MiB of HBM per device.

v0:
```python
import jax
import jax.numpy as jnp
from jax import lax
from jax.sharding import PartitionSpec as P

HEAD_DIM = 64
LANDMARKS = 64
CONV_TAPS = 33
PINV_STEPS = 6
DOCS = 8
SEQ_LEN = 1024
HIGH = lax.Precision.HIGHEST
EPSILON = 1e-05


def softmax_masked(scores, allowed):
    masked = jnp.where(allowed, scores, -1e30)
    highest = jnp.max(masked, axis=-1, keepdims=True)
    expo = jnp.exp(masked - highest)
    return expo / jnp.sum(expo, axis=-1, keepdims=True)


def layer_norm(inputs, scaling, offsets):
    centered = inputs - jnp.mean(inputs, axis=-1, keepdims=True)
    variance = jnp.mean(centered * centered, axis=-1, keepdims=True)
    return centered * lax.rsqrt(variance + EPSILON) * scaling + offsets


def gelu_exact(inputs):
    return jax.nn.gelu(inputs, approximate=False)


def nystrom(queries, key_rows, values, conv_weights, segment, landmark):
    row_count = queries.shape[0]
    head_count = queries.shape[1]
    score_scale = queries.shape[2] ** (-0.5)
    one_hot = (landmark[None, :] == jnp.arange(LANDMARKS, dtype=jnp.int32)[:, None]).astype(
        queries.dtype
    )
    pooling = one_hot / jnp.sum(one_hot, axis=1, keepdims=True)
    land_doc = jnp.arange(LANDMARKS, dtype=jnp.int32) // (LANDMARKS // DOCS)
    near_mask = segment[:, None] == land_doc[None, :]
    mark_mask = land_doc[:, None] == land_doc[None, :]
    key_marks = jnp.einsum("jt,the->jhe", pooling, key_rows, precision=HIGH)
    query_marks = jnp.einsum("jt,the->jhe", pooling, queries, precision=HIGH)
    kernel_one = softmax_masked(
        jnp.einsum("the,jhe->htj", queries, key_marks, precision=HIGH) * score_scale,
        near_mask[None],
    )
    middle = softmax_masked(
        jnp.einsum("ihe,jhe->hij", query_marks, key_marks, precision=HIGH) * score_scale,
        mark_mask[None],
    )
    kernel_last = softmax_masked(
        jnp.einsum("jhe,the->hjt", query_marks, key_rows, precision=HIGH) * score_scale,
        near_mask.T[None],
    )
    column_most = jnp.max(jnp.sum(middle, axis=1), axis=1)
    row_most = jnp.max(jnp.sum(middle, axis=2), axis=1)
    inverse = jnp.swapaxes(middle, 1, 2) / (column_most * row_most)[:, None, None]
    identity = jnp.eye(LANDMARKS, dtype=middle.dtype)
    for sweep in range(PINV_STEPS):
        product = jnp.einsum("hij,hjk->hik", middle, inverse, precision=HIGH)
        inner_term = 7.0 * identity - product
        inner_term = 15.0 * identity - jnp.einsum(
            "hij,hjk->hik", product, inner_term, precision=HIGH
        )
        inner_term = 13.0 * identity - jnp.einsum(
            "hij,hjk->hik", product, inner_term, precision=HIGH
        )
        inverse = 0.25 * jnp.einsum("hij,hjk->hik", inverse, inner_term, precision=HIGH)
    context = jnp.einsum("hjt,the->hje", kernel_last, values, precision=HIGH)
    blended = jnp.einsum("hij,hje->hie", inverse, context, precision=HIGH)
    attended = jnp.einsum("htj,hje->the", kernel_one, blended, precision=HIGH)
    half_width = CONV_TAPS // 2
    padded = jnp.pad(values, ((half_width, half_width), (0, 0), (0, 0)))
    seg_pad = jnp.pad(segment, (half_width, half_width), constant_values=-1)
    for offset in range(CONV_TAPS):
        same_doc = (seg_pad[offset : offset + row_count] == segment).astype(values.dtype)
        attended = (
            attended
            + conv_weights[:, offset][None, :, None]
            * padded[offset : offset + row_count]
            * same_doc[:, None, None]
        )
    return attended.reshape(row_count, head_count * values.shape[2])


def contract_rows(left, right):
    return lax.dot_general(
        left, right, (((0,), (0,)), ((), ())), preferred_element_type=jnp.float32
    )


def contract_cols(left, right):
    return lax.dot_general(
        left, right, (((1,), (1,)), ((), ())), preferred_element_type=jnp.float32
    )


def per_device(
    tokens,
    w_query,
    w_key,
    w_value,
    b_query,
    b_value,
    conv_taps,
    w_out,
    b_out,
    gain_one,
    shift_one,
    w_up,
    b_up,
    w_down,
    b_down,
    gain_two,
    shift_two,
    cotangent,
    segment_ids,
    landmark_ids,
):
    share_rows = tokens.shape[0] // lax.axis_size("tensor")
    first_row = lax.axis_index("tensor") * share_rows
    local_dim = w_query.shape[1]
    head_count = local_dim // HEAD_DIM
    seq_count = tokens.shape[0] // SEQ_LEN
    shaped = (seq_count, SEQ_LEN, head_count, HEAD_DIM)
    segments = segment_ids.reshape(seq_count, SEQ_LEN)
    marks = landmark_ids.reshape(seq_count, SEQ_LEN)
    queries = (jnp.dot(tokens, w_query, preferred_element_type=jnp.float32) + b_query).astype(
        jnp.bfloat16
    )
    key_rows = jnp.dot(tokens, w_key, preferred_element_type=jnp.float32).astype(jnp.bfloat16)
    values = (jnp.dot(tokens, w_value, preferred_element_type=jnp.float32) + b_value).astype(
        jnp.bfloat16
    )
    float_query = queries.astype(jnp.float32).reshape(shaped)
    float_key = key_rows.astype(jnp.float32).reshape(shaped)
    float_value = values.astype(jnp.float32).reshape(shaped)

    def attend(query_all, key_all, value_all, weights):
        return jax.vmap(nystrom, in_axes=(0, 0, 0, None, 0, 0))(
            query_all, key_all, value_all, weights, segments, marks
        )

    attended_f, attend_back = jax.vjp(attend, float_query, float_key, float_value, conv_taps)
    attended = attended_f.reshape(tokens.shape[0], local_dim).astype(jnp.bfloat16)
    summed = lax.psum_scatter(
        jnp.dot(attended, w_out, preferred_element_type=jnp.float32),
        "tensor",
        scatter_dimension=0,
        tiled=True,
    )
    own_tokens = lax.dynamic_slice_in_dim(tokens, first_row, share_rows, 0).astype(jnp.float32)
    normed, norm_back_one = jax.vjp(layer_norm, own_tokens + summed + b_out, gain_one, shift_one)
    normed_low = lax.all_gather(normed.astype(jnp.bfloat16), "tensor", axis=0, tiled=True)
    hidden = jnp.dot(normed_low, w_up, preferred_element_type=jnp.float32) + b_up
    activated_f, gelu_back = jax.vjp(gelu_exact, hidden)
    activated = activated_f.astype(jnp.bfloat16)
    branch = lax.psum_scatter(
        jnp.dot(activated, w_down, preferred_element_type=jnp.float32),
        "tensor",
        scatter_dimension=0,
        tiled=True,
    )
    output, norm_back_two = jax.vjp(layer_norm, normed + branch + b_down, gain_two, shift_two)
    grad_pre_out, grad_gain_two, grad_shift_two = norm_back_two(cotangent.astype(jnp.float32))
    grad_b_down = jnp.sum(grad_pre_out, axis=0)
    grad_branch = lax.all_gather(grad_pre_out.astype(jnp.bfloat16), "tensor", axis=0, tiled=True)
    grad_w_down = contract_rows(activated, grad_branch)
    grad_act = contract_cols(grad_branch, w_down)
    grad_hidden = gelu_back(grad_act)[0].astype(jnp.bfloat16)
    grad_w_up = contract_rows(normed_low, grad_hidden)
    grad_b_up = jnp.sum(grad_hidden, axis=0, dtype=jnp.float32)
    back_normed = lax.psum_scatter(
        contract_cols(grad_hidden, w_up).astype(jnp.bfloat16),
        "tensor",
        scatter_dimension=0,
        tiled=True,
    ).astype(jnp.float32)
    back_normed = lax.optimization_barrier(back_normed.astype(jnp.bfloat16)).astype(jnp.float32)
    grad_pre_norm, grad_gain_one, grad_shift_one = norm_back_one(grad_pre_out + back_normed)
    grad_b_out = jnp.sum(grad_pre_norm, axis=0)
    grad_summed = lax.all_gather(grad_pre_norm.astype(jnp.bfloat16), "tensor", axis=0, tiled=True)
    grad_w_out = contract_rows(attended, grad_summed)
    grad_attended = contract_cols(grad_summed, w_out).reshape(seq_count, SEQ_LEN, local_dim)
    grad_q_f, grad_k_f, grad_v_f, grad_conv = attend_back(grad_attended)
    grad_queries = grad_q_f.reshape(tokens.shape[0], local_dim).astype(jnp.bfloat16)
    grad_keys = grad_k_f.reshape(tokens.shape[0], local_dim).astype(jnp.bfloat16)
    grad_values = grad_v_f.reshape(tokens.shape[0], local_dim).astype(jnp.bfloat16)
    grad_w_query = contract_rows(tokens, grad_queries)
    grad_w_key = contract_rows(tokens, grad_keys)
    grad_w_value = contract_rows(tokens, grad_values)
    grad_b_query = jnp.sum(grad_queries, axis=0, dtype=jnp.float32)
    grad_b_value = jnp.sum(grad_values, axis=0, dtype=jnp.float32)
    total = contract_cols(grad_queries, w_query)
    total = total + contract_cols(grad_keys, w_key)
    input_grad = grad_pre_norm + lax.psum_scatter(
        (total + contract_cols(grad_values, w_value)).astype(jnp.bfloat16),
        "tensor",
        scatter_dimension=0,
        tiled=True,
    ).astype(jnp.float32)
    (
        grad_w_query,
        grad_w_key,
        grad_w_value,
        grad_b_query,
        grad_b_value,
        grad_conv,
        grad_w_out,
        grad_w_up,
        grad_w_down,
        grad_b_up,
    ) = lax.psum(
        (
            grad_w_query,
            grad_w_key,
            grad_w_value,
            grad_b_query,
            grad_b_value,
            grad_conv,
            grad_w_out,
            grad_w_up,
            grad_w_down,
            grad_b_up,
        ),
        "dp",
    )
    grad_gain_one, grad_shift_one, grad_b_out, grad_gain_two, grad_shift_two, grad_b_down = (
        lax.psum(
            (grad_gain_one, grad_shift_one, grad_b_out, grad_gain_two, grad_shift_two, grad_b_down),
            ("dp", "tensor"),
        )
    )
    return (
        output.astype(jnp.bfloat16),
        input_grad,
        grad_w_query,
        grad_w_key,
        grad_w_value,
        grad_b_query,
        grad_b_value,
        grad_conv,
        grad_w_out,
        grad_b_out,
        grad_gain_one,
        grad_shift_one,
        grad_w_up,
        grad_b_up,
        grad_w_down,
        grad_b_down,
        grad_gain_two,
        grad_shift_two,
    )


def solution(mesh):
    return jax.shard_map(
        per_device,
        mesh=mesh,
        in_specs=(
            P("dp", None),
            P(None, "tensor"),
            P(None, "tensor"),
            P(None, "tensor"),
            P("tensor"),
            P("tensor"),
            P("tensor", None),
            P("tensor", None),
            P(),
            P(),
            P(),
            P(None, "tensor"),
            P("tensor"),
            P("tensor", None),
            P(),
            P(),
            P(),
            P(("dp", "tensor"), None),
            P("dp"),
            P("dp"),
        ),
        out_specs=(
            P(("dp", "tensor"), None),
            P(("dp", "tensor"), None),
            P(None, "tensor"),
            P(None, "tensor"),
            P(None, "tensor"),
            P("tensor"),
            P("tensor"),
            P("tensor", None),
            P("tensor", None),
            P(),
            P(),
            P(),
            P(None, "tensor"),
            P("tensor"),
            P("tensor", None),
            P(),
            P(),
            P(),
        ),
        check_vma=False,
    )
```

profile of v0, /device:TPU:0, one launch (start us, length us, event | category | flops | bytes accessed | tf_op | source)
XLA Modules:
  0.0 814.8 jit_solution(1764736523739853846)
XLA Ops:
  7.3 2.2 slice_reduce_fusion.31
  9.5 2.4 slice_reduce_fusion.32
  17.3 3.2 fusion.7
  22.0 2.5 reshape.559
  24.8 3.1 fusion.6
  28.8 4.2 convolution_convert_fusion.1
  33.1 3.0 reshape.557
  61.8 16.0 %add_convert_fusion.3 = bf16[2,1024,3,64]{1,3,2,0:T(8,128)(2,1)S(1)} fusion(f32[2,1024,3,64]{1,3,2,0:T(8,128)S(1)} %copy.171, f32[2,3,64,64]{3,2,1,0:T(8,128)S(1)} %fusion.182, f32[2,1024]{1,0:T(2,128)S(1)} %copy-done.179, f32[3]{0:T(128)} %get-tuple-element.144, f32[2,1024]{1,0:T(2,128)S(1)} %copy-done.143, f32[3]{0:T(128)} %get-tuple-element.145, ...), kind=kOutput, calls=%fused_computation.126 | convolution fusion | flops 341704704 | bytes 4342156 | tf_op jit(solution)/shard_map/jvp(vmap(htj,hje->the))/dot_general | solution.py:74
  78.9 3.7 fusion.183
  82.7 61.1 %reduce-scatter.5.cloned.1.call-done = f32[512,768]{1,0:T(8,128)} async-done(((f32[2048,768]{1,0:T(8,128)}), f32[512,768]{1,0:T(8,128)}) %reduce-scatter.5.cloned.1.call-update) | async-done | bytes 1572880 | tf_op jit(solution)/shard_map/reduce_scatter | solution.py:149
  147.7 28.6 %all-gather.4.cloned.1.call-done = bf16[2048,768]{1,0:T(8,128)(2,1)} async-done(((bf16[512,768]{1,0:T(8,128)(2,1)}), bf16[2048,768]{1,0:T(8,128)(2,1)}) %all-gather.4.cloned.1.call-update) | async-done | bytes 3145744 | tf_op jit(solution)/shard_map/all_gather | solution.py:157
  176.3 18.7 %multiply_convert_fusion = (bf16[2048,768]{1,0:T(8,128)(2,1)S(1)}, f32[2048,768]{1,0:T(8,128)}, f32[2048,768]{1,0:T(8,128)}) fusion(f32[768]{0:T(1024)S(1)} %copy-done.314, bf16[2048,768]{1,0:T(8,128)(2,1)} %all-gather.4.cloned.1.call-done, bf16[768,768]{1,0:T(8,128)(2,1)S(1)} %copy-done), kind=kOutput, calls=%fused_computation.5 | convolution fusion | flops 2519728128 | bytes 20057088 | tf_op jit(solution)/shard_map/dot_general | solution.py:158
  196.7 4.5 fusion.184
  201.2 58.5 %reduce-scatter.7.cloned.1.call-done = f32[512,768]{1,0:T(8,128)} async-done(((f32[2048,768]{1,0:T(8,128)}), f32[512,768]{1,0:T(8,128)}) %reduce-scatter.7.cloned.1.call-update) | async-done | bytes 1572880 | tf_op jit(solution)/shard_map/reduce_scatter | solution.py:161
  264.0 2.1 fusion.171
  266.2 2.4 add_convert_fusion.5
  268.7 28.7 %all-gather.6.cloned.1.call-done = bf16[2048,768]{1,0:T(8,128)(2,1)} async-done(((bf16[512,768]{1,0:T(8,128)(2,1)}), bf16[2048,768]{1,0:T(8,128)(2,1)}) %all-gather.6.cloned.1.call-update) | async-done | bytes 3145744 | tf_op jit(solution)/shard_map/all_gather | solution.py:170
  297.3 11.1 %convert_reduce_fusion = (f32[768]{0:T(1024)}, bf16[2048,768]{1,0:T(8,128)(2,1)S(1)}) fusion(f32[2048,768]{1,0:T(8,128)} %get-tuple-element.189, f32[2048,768]{1,0:T(8,128)} %get-tuple-element.276, f32[768]{0:T(1024)S(1)} %copy-done.314, bf16[2048,768]{1,0:T(8,128)(2,1)} %all-gather.6.cloned.1.call-done, bf16[768,768]{1,0:T(8,128)(2,1)} %param.33), kind=kOutput, calls=%fused_computation.2 | convolution fusion | flops 2442657024 | bytes 20060160 | tf_op jit(solution)/shard_map/dot_general | solution.py:96
  310.1 4.0 convolution_convert_fusion
  314.2 38.1 %reduce-scatter.9.cloned.1.call-done = bf16[512,768]{1,0:T(8,128)(2,1)} async-done(((bf16[2048,768]{1,0:T(8,128)(2,1)}), bf16[512,768]{1,0:T(8,128)(2,1)}) %reduce-scatter.9.cloned.1.call-update) | async-done | bytes 786448 | tf_op jit(solution)/shard_map/reduce_scatter | solution.py:176
  352.2 3.2 multiply_reduce_fusion
  355.4 3.3 fusion.170
  358.8 3.2 add_reduce_fusion
  365.6 25.1 %all-gather.8.cloned.1.call-done = bf16[2048,768]{1,0:T(8,128)(2,1)} async-done(((bf16[512,768]{1,0:T(8,128)(2,1)}), bf16[2048,768]{1,0:T(8,128)(2,1)}) %all-gather.8.cloned.1.call-update) | async-done | bytes 3145744 | tf_op jit(solution)/shard_map/all_gather | solution.py:185
  390.7 3.7 multiply_reduce_fusion.17
  395.8 3.5 fusion.41
  419.8 6.4 multiply_reduce_fusion.30
  426.3 5.1 multiply_multiply_fusion.17
  431.7 6.3 multiply_multiply_fusion.36
  438.2 5.6 multiply_multiply_fusion.26
  456.6 2.5 fusion.101
  459.2 2.6 convert_reduce_fusion.5
  462.8 3.5 convert_reduce_fusion.3
  473.1 2.2 fusion.14
  476.3 3.7 fusion.200
  480.1 3.7 fusion.199
  483.8 20.5 %pad_add_fusion = f32[2,1056,3,64]{1,3,2,0:T(8,128)} fusion(f32[2,1024,3,64]{1,3,2,0:T(8,128)} %get-tuple-element.229, f32[2,1024,3,64]{1,3,2,0:T(8,128)} %get-tuple-element.228, f32[2,1024,3,64]{1,3,2,0:T(8,128)} %get-tuple-element.227, f32[2,1024,3,64]{1,3,2,0:T(8,128)} %get-tuple-element.226, f32[2,1024,3,64]{1,3,2,0:T(8,128)} %get-tuple-element.225, ...), kind=kLoop, calls=%fused_computation.32 | loop fusion | flops 10543104 | bytes 44089344 | tf_op jit(solution)/shard_map/transpose(jvp(vmap()))/add_any | solution.py:83
  504.4 6.8 convert_reduce_fusion.2
  513.2 2.7 add_convert_fusion
  516.0 7.1 fusion.203
  523.1 4.2 fusion.202
  535.2 40.7 %all-reduce.68 = (f32[768]{0:T(1024)}, f32[768]{0:T(1024)}, f32[768]{0:T(1024)}, f32[768]{0:T(1024)}, f32[768]{0:T(1024)}, /*index=5*/f32[768]{0:T(1024)}) all-reduce(f32[768]{0:T(1024)S(1)} %copy-done.242, f32[768]{0:T(1024)S(1)} %copy-done.252, f32[768]{0:T(1024)S(1)} %copy-done.253, ...), channel_id=1, replica_groups=mesh['dp'=8,'tensor'=4] {'dp','tensor'}, use_global_device_ids=true, to_apply=%region_79.80 | all-reduce | flops 4608 | bytes 36864 | tf_op jit(solution)/shard_map/psum | solution.py:232
  576.5 4.0 multiply_reduce_fusion.31
  580.6 4.0 multiply_reduce_fusion.32
  584.8 4.0 multiply_reduce_fusion.33
  589.0 39.9 %all-reduce.69 = (f32[192]{0:T(256)}, f32[192]{0:T(256)}, f32[3,33]{0,1:T(8,128)S(1)}, f32[768]{0:T(1024)}) all-reduce(f32[192]{0:T(256)S(1)} %reduce_sum.660, f32[192]{0:T(256)S(1)} %reduce_sum.665, f32[3,33]{0,1:T(8,128)S(1)} %pad_add_fusion.7, f32[768]{0:T(1024)S(1)} %copy-done.268), channel_id=1, replica_groups=mesh['dp'=8,'tensor'=4] {'dp'}, use_global_device_ids=true, to_apply=%region_39.40 | all-reduce | flops 1251 | bytes 10008 | tf_op jit(solution)/shard_map/psum | solution.py:216
  629.5 3.0 convert_add_fusion
  632.5 166.6 %all-reduce.73.cloned.1.call-done = (f32[768,192]{0,1:T(8,128)}, f32[768,192]{0,1:T(8,128)}, f32[768,192]{0,1:T(8,128)}, f32[192,768]{1,0:T(8,128)}, f32[768,768]{1,0:T(8,128)}, /*index=5*/f32[768,768]{1,0:T(8,128)}) async-done(((f32[768,192]{0,1:T(8,128)}, f32[768,192]{0,1:T(8,128)}, f32[768,192]{0,1:T(8,128)}, f32[192,768]{1,0:T(8,128)}, f32[768,768]{1,0:T(8,128)}, /*index=5*/f32[768,768]{1,0:T(8,128)}), ...) | async-done | bytes 7077904 | tf_op jit(solution)/shard_map/psum | solution.py:216
  (828 shorter events, 110.0 us)
Async XLA Ops:
  7.2 169.1 %copy-start = (bf16[768,768]{1,0:T(8,128)(2,1)S(1)}, bf16[768,768]{1,0:T(8,128)(2,1)}, u32[]{:S(2)}) copy-start(bf16[768,768]{1,0:T(8,128)(2,1)} %param.31) | copy-start | bytes 3538948
  7.2 136.6 %reduce-scatter.5.cloned.1.call-start = ((), (), s32[]{:S(2)}) async-start(), calls=%async_computation.4 | async-start | bytes 7864320 | tf_op jit(solution)/shard_map/reduce_scatter | solution.py:149
  11.9 37.9 %copy-start.88 = (f32[64,64]{1,0:T(8,128)}, f32[64,64]{1,0:T(8,128)S(1)}, u32[]{:S(2)}) copy-start(f32[64,64]{1,0:T(8,128)S(1)} %fusion.149) | copy-start | bytes 49156
  11.9 37.5 %copy-start.36 = (f32[64,64]{1,0:T(8,128)}, f32[64,64]{1,0:T(8,128)S(1)}, u32[]{:S(2)}) copy-start(f32[64,64]{1,0:T(8,128)S(1)} %get-tuple-element.291) | copy-start | bytes 49156
  11.9 37.5 %copy-start.90 = (f32[64,64]{1,0:T(8,128)}, f32[64,64]{1,0:T(8,128)S(1)}, u32[]{:S(2)}) copy-start(f32[64,64]{1,0:T(8,128)S(1)} %get-tuple-element.292) | copy-start | bytes 49156
  24.5 12.7 %copy-start.234 = (s32[2,1024]{1,0:T(2,128)}, s32[2,1024]{1,0:T(2,128)S(1)}, u32[]{:S(2)}) copy-start(s32[2,1024]{1,0:T(2,128)S(1)} %eq.252) | copy-start | bytes 24580
  24.7 12.6 %copy-start.307 = (f32[2,64]{1,0:T(2,128)}, f32[2,64]{1,0:T(2,128)S(1)}, u32[]{:S(2)}) copy-start(f32[2,64]{1,0:T(2,128)S(1)} %convert_reduce_fusion.6) | copy-start | bytes 1540
  24.8 18.3 %copy-start.257 = (pred[64,64]{1,0:T(8,128)(4,1)}, pred[64,64]{1,0:T(8,128)(4,1)S(1)}, u32[]{:S(2)}) copy-start(pred[64,64]{1,0:T(8,128)(4,1)S(1)} %copy.157) | copy-start | bytes 12292
  28.8 7.2 copy-start.97
  53.8 6.6 copy-start.86
  61.1 16.7 %copy-start.123 = (f32[2,3,64,64]{3,2,1,0:T(8,128)}, f32[2,3,64,64]{3,2,1,0:T(8,128)S(1)}, u32[]{:S(2)}) copy-start(f32[2,3,64,64]{3,2,1,0:T(8,128)S(1)} %fusion.182) | copy-start | bytes 294916
  61.4 303.6 %copy-start.116 = (f32[2,3,1024]{2,1,0:T(4,128)}, f32[2,3,1024]{2,1,0:T(4,128)S(1)}, u32[]{:S(2)}) copy-start(f32[2,3,1024]{2,1,0:T(4,128)S(1)} %fusion.65) | copy-start | bytes 73732
  82.6 61.2 %copy-start.259 = (f32[768]{0:T(1024)S(1)}, f32[768]{0:T(1024)}, u32[]{:S(2)}) copy-start(f32[768]{0:T(1024)} %param.28) | copy-start | bytes 9220
  82.6 93.7 %all-gather.4.cloned.1.call-start = ((), (), s32[]{:S(2)}) async-start(), calls=%async_computation.5 | async-start | bytes 3932160 | tf_op jit(solution)/shard_map/all_gather | solution.py:157
  146.4 29.9 %copy-start.314 = (f32[768]{0:T(1024)S(1)}, f32[768]{0:T(1024)}, u32[]{:S(2)}) copy-start(f32[768]{0:T(1024)} %param.32) | copy-start | bytes 9220
  147.6 112.1 %reduce-scatter.7.cloned.1.call-start = ((), (), s32[]{:S(2)}) async-start(), calls=%async_computation.6 | async-start | bytes 7864320 | tf_op jit(solution)/shard_map/reduce_scatter | solution.py:161
  176.3 20.4 %copy-start.313 = (bf16[768,768]{1,0:T(8,128)(2,1)S(1)}, bf16[768,768]{1,0:T(8,128)(2,1)}, u32[]{:S(2)}) copy-start(bf16[768,768]{1,0:T(8,128)(2,1)} %param.33) | copy-start | bytes 3538948
  201.2 58.5 %copy-start.269 = (f32[768]{0:T(1024)S(1)}, f32[768]{0:T(1024)}, u32[]{:S(2)}) copy-start(f32[768]{0:T(1024)} %param.34) | copy-start | bytes 9220
  201.2 96.2 %all-gather.6.cloned.1.call-start = ((), (), s32[]{:S(2)}) async-start(), calls=%async_computation.7 | async-start | bytes 3932160 | tf_op jit(solution)/shard_map/all_gather | solution.py:170
  268.6 83.6 %reduce-scatter.9.cloned.1.call-start = ((), (), s32[]{:S(2)}) async-start(), calls=%async_computation.8 | async-start | bytes 3932160 | tf_op jit(solution)/shard_map/reduce_scatter | solution.py:176
  314.1 76.6 %all-gather.8.cloned.1.call-start = ((), (), s32[]{:S(2)}) async-start(), calls=%async_computation.9 | async-start | bytes 3932160 | tf_op jit(solution)/shard_map/all_gather | solution.py:185
  358.8 31.9 %copy-start.11 = (bf16[2048,192]{0,1:T(8,128)(2,1)S(1)}, bf16[2048,192]{0,1:T(8,128)(2,1)}, u32[]{:S(2)}) copy-start(bf16[2048,192]{0,1:T(8,128)(2,1)} %copy-done.10) | copy-start | bytes 2359300
  358.8 31.9 %copy-start.93 = (bf16[192,768]{1,0:T(8,128)(2,1)S(1)}, bf16[192,768]{1,0:T(8,128)(2,1)}, u32[]{:S(2)}) copy-start(bf16[192,768]{1,0:T(8,128)(2,1)} %param.27) | copy-start | bytes 884740
  362.1 267.4 %reduce-scatter.11.cloned.1.call-start = ((), (), s32[]{:S(2)}) async-start(), calls=%async_computation.10 | async-start | bytes 3932160 | tf_op jit(solution)/shard_map/reduce_scatter | solution.py:199
  400.3 47.6 %copy-start.106 = (f32[2,3,64,64]{3,2,1,0:T(8,128)}, f32[2,3,64,64]{3,2,1,0:T(8,128)S(1)}, u32[]{:S(2)}) copy-start(f32[2,3,64,64]{3,2,1,0:T(8,128)S(1)} %fusion.185) | copy-start | bytes 294916
  471.5 8.5 %copy-start.22 = (bf16[24,8,2,1024]{3,1,2,0:T(8,128)(2,1)}, bf16[24,8,2,1024]{3,1,2,0:T(8,128)(2,1)S(1)}, u32[]{:S(2)}) copy-start(bf16[24,8,2,1024]{3,1,2,0:T(8,128)(2,1)S(1)} %copy.273) | copy-start | bytes 2359300
  483.8 20.5 %copy-start.8 = (f32[2,3,64,1024]{3,2,1,0:T(8,128)S(1)}, f32[2,3,64,1024]{3,2,1,0:T(8,128)}, u32[]{:S(2)}) copy-start(f32[2,3,64,1024]{3,2,1,0:T(8,128)} %copy-done.6) | copy-start | bytes 4718596
  483.8 20.6 %copy-start.107 = (f32[2,3,64,64]{3,2,1,0:T(8,128)S(1)}, f32[2,3,64,64]{3,2,1,0:T(8,128)}, u32[]{:S(2)}) copy-start(f32[2,3,64,64]{3,2,1,0:T(8,128)} %copy-done.106) | copy-start | bytes 294916
  483.8 20.6 %copy-start.208 = (f32[2,3,64]{2,1,0:T(4,128)S(1)}, f32[2,3,64]{2,1,0:T(4,128)}, u32[]{:S(2)}) copy-start(f32[2,3,64]{2,1,0:T(4,128)} %copy-done.206) | copy-start | bytes 4612
  483.8 20.6 %copy-start.212 = (f32[2,3,64]{2,1,0:T(4,128)S(1)}, f32[2,3,64]{2,1,0:T(4,128)}, u32[]{:S(2)}) copy-start(f32[2,3,64]{2,1,0:T(4,128)} %copy-done.209) | copy-start | bytes 4612
  504.3 8.8 %slice-start = ((s8[6291456]{0:T(1024)(128)(4,1)}), s8[4194304]{0:T(1024)(128)(4,1)S(1)}, s32[]{:S(2)}) async-start(s8[6291456]{0:T(1024)(128)(4,1)} %bitcast.353), calls=%async_computation.12 | async-start | bytes 8388608
  504.4 8.8 %slice-start.1 = ((s8[6291456]{0:T(1024)(128)(4,1)}), s8[2097152]{0:T(1024)(128)(4,1)S(1)}, s32[]{:S(2)}) async-start(s8[6291456]{0:T(1024)(128)(4,1)} %bitcast.353), calls=%async_computation.13 | async-start | bytes 4194304
  504.4 8.8 %copy-start.4 = (f32[2048,768]{1,0:T(8,128)S(1)}, f32[2048,768]{1,0:T(8,128)}, u32[]{:S(2)}) copy-start(f32[2048,768]{1,0:T(8,128)} %fusion.199) | copy-start | bytes 18874372
  516.0 283.2 %all-reduce.73.cloned.1.call-start = ((), (), s32[]{:S(2)}) async-start(), calls=%async_computation.11 | async-start | bytes 14155776 | tf_op jit(solution)/shard_map/psum | solution.py:216
  516.0 7.1 copy-start.312
  516.0 7.1 copy-start.318
  534.5 41.4 %copy-start.261 = (f32[192]{0:T(256)S(1)}, f32[192]{0:T(256)}, u32[]{:S(2)}) copy-start(f32[192]{0:T(256)} %get-tuple-element.287) | copy-start | bytes 2308
  534.5 41.5 %copy-start.255 = (f32[3,64]{1,0:T(4,128)S(1)}, f32[3,64]{1,0:T(4,128)}, u32[]{:S(2)}) copy-start(f32[3,64]{1,0:T(4,128)} %get-tuple-element.283) | copy-start | bytes 2308
  534.5 41.8 %copy-start.148 = (f32[2,1024]{1,0:T(2,128)S(1)}, f32[2,1024]{1,0:T(2,128)}, u32[]{:S(2)}) copy-start(f32[2,1024]{1,0:T(2,128)} %get-tuple-element.244) | copy-start | bytes 24580
  534.5 41.8 %copy-start.151 = (f32[2,1024]{1,0:T(2,128)S(1)}, f32[2,1024]{1,0:T(2,128)}, u32[]{:S(2)}) copy-start(f32[2,1024]{1,0:T(2,128)} %get-tuple-element.245) | copy-start | bytes 24580
  534.5 41.8 %copy-start.154 = (f32[2,1024]{1,0:T(2,128)S(1)}, f32[2,1024]{1,0:T(2,128)}, u32[]{:S(2)}) copy-start(f32[2,1024]{1,0:T(2,128)} %get-tuple-element.246) | copy-start | bytes 24580
  534.5 41.8 %copy-start.157 = (f32[2,1024]{1,0:T(2,128)S(1)}, f32[2,1024]{1,0:T(2,128)}, u32[]{:S(2)}) copy-start(f32[2,1024]{1,0:T(2,128)} %get-tuple-element.247) | copy-start | bytes 24580
  534.6 41.8 %copy-start.160 = (f32[2,1024]{1,0:T(2,128)S(1)}, f32[2,1024]{1,0:T(2,128)}, u32[]{:S(2)}) copy-start(f32[2,1024]{1,0:T(2,128)} %get-tuple-element.248) | copy-start | bytes 24580
  534.6 41.8 %copy-start.163 = (f32[2,1024]{1,0:T(2,128)S(1)}, f32[2,1024]{1,0:T(2,128)}, u32[]{:S(2)}) copy-start(f32[2,1024]{1,0:T(2,128)} %get-tuple-element.249) | copy-start | bytes 24580
  534.6 41.8 %copy-start.166 = (f32[2,1024]{1,0:T(2,128)S(1)}, f32[2,1024]{1,0:T(2,128)}, u32[]{:S(2)}) copy-start(f32[2,1024]{1,0:T(2,128)} %get-tuple-element.236) | copy-start | bytes 24580
  534.6 41.8 %copy-start.169 = (f32[2,1024]{1,0:T(2,128)S(1)}, f32[2,1024]{1,0:T(2,128)}, u32[]{:S(2)}) copy-start(f32[2,1024]{1,0:T(2,128)} %get-tuple-element.241) | copy-start | bytes 24580
  534.6 41.8 %copy-start.172 = (f32[2,1024]{1,0:T(2,128)S(1)}, f32[2,1024]{1,0:T(2,128)}, u32[]{:S(2)}) copy-start(f32[2,1024]{1,0:T(2,128)} %get-tuple-element.242) | copy-start | bytes 24580
  584.8 44.7 %copy-start.237 = (f32[512]{0:T(512)S(1)}, f32[512]{0:T(512)}, u32[]{:S(2)}) copy-start(f32[512]{0:T(512)} %copy-done.236) | copy-start | bytes 6148
  (281 other events, 787.9 us)
Sparse Core Ops, SparseCore 0:
  82.7 61.0 reduce-scatter.4
  147.7 28.5 all-gather.3
  201.3 58.3 reduce-scatter.6
  268.7 28.5 all-gather.5
  314.2 37.9 reduce-scatter.8
  362.2 28.5 all-gather.7
  516.1 38.6 reduce-scatter.10
  561.0 238.0 all-reduce.72
where the time goes:
time: 822 us; the launch traced here: 815 us
  waiting for transfers between devices  407 us (50%)
  matrix products  168 us (20%)
  other arithmetic  92.5 us (11%)
  blocking collectives  80.6 us (10%)
  local copies, waits for them, and re-layouts  46.4 us (6%)
  between operations  19.5 us (2%)
    psum x1, waiting for transfers between devices, per_device(): lax.psum((grad_w_query, grad_w_key, grad_w_value, grad_b_query, grad_b_va...  167 us
    reduce_scatter x1, waiting for transfers between devices, per_device(): lax.psum_scatter(jnp.dot(attended, w_out, preferred_element_type=jnp.floa...  61.1 us
    reduce_scatter x1, waiting for transfers between devices, per_device(): lax.psum_scatter(jnp.dot(activated, w_down, preferred_element_type=jnp.fl...  58.5 us
    psum x1, blocking collectives, per_device(): lax.psum((grad_gain_one, grad_shift_one, grad_b_out, grad_gain_two, grad_...  40.7 us
    psum x1, blocking collectives, per_device(): lax.psum((grad_w_query, grad_w_key, grad_w_value, grad_b_query, grad_b_va...  39.9 us
    reduce_scatter x1, waiting for transfers between devices, per_device(): lax.psum_scatter(contract_cols(grad_hidden, w_up).astype(jnp.bfloat16), '...  38.1 us
    dot_general x6, matrix products, contract_cols(): lax.dot_general(left, right, (((1,), (1,)), ((), ())), preferred_element_...  29 us
    all_gather x1, waiting for transfers between devices, per_device(): lax.all_gather(grad_pre_out.astype(jnp.bfloat16), 'tensor', axis=0, tiled...  28.7 us
  transfers between devices with their start and end apart: 8, of which 7 were waited for; matrix products, arithmetic and copies ran while one was open for 5% of the time, Pallas kernels for 0%

commit v1 on v0

--- a/solution.py
+++ b/solution.py
@@ -182,7 +182,35 @@
     back_normed = lax.optimization_barrier(back_normed.astype(jnp.bfloat16)).astype(jnp.float32)
     grad_pre_norm, grad_gain_one, grad_shift_one = norm_back_one(grad_pre_out + back_normed)
     grad_b_out = jnp.sum(grad_pre_norm, axis=0)
-    grad_summed = lax.all_gather(grad_pre_norm.astype(jnp.bfloat16), "tensor", axis=0, tiled=True)
+
+    def spread_panels(inp, device_axis):
+        moved, inter, upper = (
+            lax.axis_size(device_axis),
+            lax.axis_index(device_axis),
+            inp.shape[0],
+        )
+        found = [c * moved if k0 == 0 else c for k0, c in enumerate(inp.shape)]
+        block_out = lax.dynamic_update_slice_in_dim(
+            jnp.zeros(found, inp.dtype), inp, inter * upper, axis=0
+        )
+        parts_out = b_next = inp
+        for j in range(1, moved // 2 + 1):
+            parts_out = lax.ppermute(
+                parts_out, device_axis, [(k0, (k0 + 1) % moved) for k0 in range(moved)]
+            )
+            block_out = lax.dynamic_update_slice_in_dim(
+                block_out, parts_out, (inter - j) % moved * upper, axis=0
+            )
+            if 2 * j < moved:
+                b_next = lax.ppermute(
+                    b_next, device_axis, [(k0, (k0 - 1) % moved) for k0 in range(moved)]
+                )
+                block_out = lax.dynamic_update_slice_in_dim(
+                    block_out, b_next, (inter + j) % moved * upper, axis=0
+                )
+        return block_out
+
+    grad_summed = spread_panels(grad_pre_norm.astype(jnp.bfloat16), "tensor")
     grad_w_out = contract_rows(attended, grad_summed)
     grad_attended = contract_cols(grad_summed, w_out).reshape(seq_count, SEQ_LEN, local_dim)
     grad_q_f, grad_k_f, grad_v_f, grad_conv = attend_back(grad_attended)

time: 822 us -> 823 us (level)
    all_gather x1 -> x0, waiting for transfers between devices: 25.1 us -> none  [per_device(): lax.all_gather(grad_pre_norm.astype(jnp.bfloat16), 'tensor', axis=0, tile...]
    ppermute x0 -> x3, waiting for transfers between devices: none -> 21.9 us  [the longest x2 21.9 us: spread_panels(): lax.ppermute(parts_out, device_axis, [(k0, (k0 + 1) % moved) for k0 in ra...]
    unnamed x653 -> x649, local copies, waits for them, and re-layouts: 24.1 us -> 25.1 us
  transfers between devices with their start and end apart: 8 -> 10, of which waited for: 7 -> 8; matrix products, arithmetic and copies ran while one was open for 5% -> 5% of each run, Pallas kernels for 0% -> 0%
where the time goes in v1:
time: 823 us; the launch traced here: 816 us
  waiting for transfers between devices  403 us (49%)
  matrix products  167 us (20%)
  other arithmetic  91 us (11%)
  blocking collectives  80.1 us (10%)
  local copies, waits for them, and re-layouts  52.4 us (6%)
  between operations  19.5 us (2%)
    psum x1, waiting for transfers between devices, per_device(): lax.psum((grad_w_query, grad_w_key, grad_w_value, grad_b_query, grad_b_va...  166 us
    reduce_scatter x1, waiting for transfers between devices, per_device(): lax.psum_scatter(jnp.dot(attended, w_out, preferred_element_type=jnp.floa...  61.1 us
    reduce_scatter x1, waiting for transfers between devices, per_device(): lax.psum_scatter(jnp.dot(activated, w_down, preferred_element_type=jnp.fl...  58.5 us
    psum x1, blocking collectives, per_device(): lax.psum((grad_gain_one, grad_shift_one, grad_b_out, grad_gain_two, grad_...  41.7 us
    psum x1, blocking collectives, per_device(): lax.psum((grad_w_query, grad_w_key, grad_w_value, grad_b_query, grad_b_va...  38.5 us
    reduce_scatter x1, waiting for transfers between devices, per_device(): lax.psum_scatter(contract_cols(grad_hidden, w_up).astype(jnp.bfloat16), '...  38.1 us
    all_gather x1, waiting for transfers between devices, per_device(): lax.all_gather(grad_pre_out.astype(jnp.bfloat16), 'tensor', axis=0, tiled...  28.7 us
    all_gather x1, waiting for transfers between devices, per_device(): lax.all_gather(normed.astype(jnp.bfloat16), 'tensor', axis=0, tiled=True)  28.6 us
  transfers between devices with their start and end apart: 10, of which 8 were waited for; matrix products, arithmetic and copies ran while one was open for 5% of the time, Pallas kernels for 0%

profile of v1, /device:TPU:0, one launch (start us, length us, event | category | flops | bytes accessed | tf_op | source)
XLA Modules:
  0.0 815.5 jit_solution(15090948292566080242)
XLA Ops:
  7.3 2.2 slice_reduce_fusion.31
  9.5 2.4 slice_reduce_fusion.32
  17.4 3.2 fusion.7
  22.1 2.5 reshape.559
  24.9 3.1 fusion.6
  28.9 4.2 convolution_convert_fusion.1
  33.1 2.7 reshape.557
  62.2 16.0 %add_convert_fusion.3 = bf16[2,1024,3,64]{1,3,2,0:T(8,128)(2,1)S(1)} fusion(f32[2,1024,3,64]{1,3,2,0:T(8,128)S(1)} %copy.171, f32[2,3,64,64]{3,2,1,0:T(8,128)S(1)} %fusion.182, f32[2,1024]{1,0:T(2,128)S(1)} %copy-done.182, f32[3]{0:T(128)} %get-tuple-element.144, f32[2,1024]{1,0:T(2,128)S(1)} %copy-done.146, f32[3]{0:T(128)} %get-tuple-element.145, ...), kind=kOutput, calls=%fused_computation.126 | convolution fusion | flops 341704704 | bytes 4342156 | tf_op jit(solution)/shard_map/jvp(vmap(htj,hje->the))/dot_general | solution.py:74
  79.2 3.7 fusion.183
  83.0 61.1 %reduce-scatter.5.cloned.1.call-done = f32[512,768]{1,0:T(8,128)} async-done(((f32[2048,768]{1,0:T(8,128)}), f32[512,768]{1,0:T(8,128)}) %reduce-scatter.5.cloned.1.call-update) | async-done | bytes 1572880 | tf_op jit(solution)/shard_map/reduce_scatter | solution.py:149
  148.0 28.6 %all-gather.3.cloned.1.call-done = bf16[2048,768]{1,0:T(8,128)(2,1)} async-done(((bf16[512,768]{1,0:T(8,128)(2,1)}), bf16[2048,768]{1,0:T(8,128)(2,1)}) %all-gather.3.cloned.1.call-update) | async-done | bytes 3145744 | tf_op jit(solution)/shard_map/all_gather | solution.py:157
  176.7 18.7 %multiply_convert_fusion = (bf16[2048,768]{1,0:T(8,128)(2,1)S(1)}, f32[2048,768]{1,0:T(8,128)}, f32[2048,768]{1,0:T(8,128)}) fusion(f32[768]{0:T(1024)S(1)} %copy-done.312, bf16[2048,768]{1,0:T(8,128)(2,1)} %all-gather.3.cloned.1.call-done, bf16[768,768]{1,0:T(8,128)(2,1)S(1)} %copy-done), kind=kOutput, calls=%fused_computation.5 | convolution fusion | flops 2519728128 | bytes 20057088 | tf_op jit(solution)/shard_map/dot_general | solution.py:158
  197.0 4.5 fusion.184
  201.6 58.5 %reduce-scatter.7.cloned.1.call-done = f32[512,768]{1,0:T(8,128)} async-done(((f32[2048,768]{1,0:T(8,128)}), f32[512,768]{1,0:T(8,128)}) %reduce-scatter.7.cloned.1.call-update) | async-done | bytes 1572880 | tf_op jit(solution)/shard_map/reduce_scatter | solution.py:161
  266.5 2.4 add_convert_fusion.5
  269.0 28.7 %all-gather.5.cloned.1.call-done = bf16[2048,768]{1,0:T(8,128)(2,1)} async-done(((bf16[512,768]{1,0:T(8,128)(2,1)}), bf16[2048,768]{1,0:T(8,128)(2,1)}) %all-gather.5.cloned.1.call-update) | async-done | bytes 3145744 | tf_op jit(solution)/shard_map/all_gather | solution.py:170
  297.7 11.1 %convert_reduce_fusion = (f32[768]{0:T(1024)}, bf16[2048,768]{1,0:T(8,128)(2,1)S(1)}) fusion(f32[2048,768]{1,0:T(8,128)} %get-tuple-element.191, f32[2048,768]{1,0:T(8,128)} %get-tuple-element.278, f32[768]{0:T(1024)S(1)} %copy-done.312, bf16[2048,768]{1,0:T(8,128)(2,1)} %all-gather.5.cloned.1.call-done, bf16[768,768]{1,0:T(8,128)(2,1)} %param.33), kind=kOutput, calls=%fused_computation.2 | convolution fusion | flops 2442657024 | bytes 20060160 | tf_op jit(solution)/shard_map/dot_general | solution.py:96
  310.5 4.4 convolution_convert_fusion
  314.9 38.1 %reduce-scatter.9.cloned.1.call-done = bf16[512,768]{1,0:T(8,128)(2,1)} async-done(((bf16[2048,768]{1,0:T(8,128)(2,1)}), bf16[512,768]{1,0:T(8,128)(2,1)}) %reduce-scatter.9.cloned.1.call-update) | async-done | bytes 786448 | tf_op jit(solution)/shard_map/reduce_scatter | solution.py:176
  353.0 3.2 multiply_reduce_fusion
  356.2 2.3 fusion.170
  362.5 16.6 %collective-permute-done = bf16[512,768]{1,0:T(8,128)(2,1)} collective-permute-done((bf16[512,768]{1,0:T(8,128)(2,1)}, bf16[512,768]{1,0:T(8,128)(2,1)}, u32[]{:S(2)}, u32[]{:S(2)}) %collective-permute-start) | collective-permute-done | bytes 786464 | tf_op jit(solution)/shard_map/ppermute | solution.py:198
  385.5 5.3 collective-permute-done.2
  392.1 2.9 multiply_reduce_fusion.17
  394.9 2.7 reshape_reshape.3
  397.7 2.9 fusion.41
  421.0 6.3 multiply_reduce_fusion.30
  427.5 5.1 multiply_multiply_fusion.17
  432.9 6.3 multiply_multiply_fusion.36
  439.4 5.6 multiply_multiply_fusion.26
  457.8 2.5 fusion.101
  460.4 2.6 convert_reduce_fusion.5
  463.9 3.5 convert_reduce_fusion.3
  474.3 2.2 fusion.14
  477.5 3.7 fusion.200
  481.3 3.7 fusion.199
  485.0 20.5 %pad_add_fusion = f32[2,1056,3,64]{1,3,2,0:T(8,128)} fusion(f32[2,1024,3,64]{1,3,2,0:T(8,128)} %get-tuple-element.231, f32[2,1024,3,64]{1,3,2,0:T(8,128)} %get-tuple-element.230, f32[2,1024,3,64]{1,3,2,0:T(8,128)} %get-tuple-element.229, f32[2,1024,3,64]{1,3,2,0:T(8,128)} %get-tuple-element.228, f32[2,1024,3,64]{1,3,2,0:T(8,128)} %get-tuple-element.227, ...), kind=kLoop, calls=%fused_computation.32 | loop fusion | flops 10543104 | bytes 44089344 | tf_op jit(solution)/shard_map/transpose(jvp(vmap()))/add_any | solution.py:83
  505.6 6.8 convert_reduce_fusion.2
  514.4 2.7 add_convert_fusion
  517.2 7.1 fusion.203
  524.3 4.2 fusion.202
  536.8 4.2 multiply_reduce_fusion.31
  541.2 4.0 multiply_reduce_fusion.32
  545.4 4.0 multiply_reduce_fusion.33
  549.5 38.5 %all-reduce.69 = (f32[192]{0:T(256)}, f32[192]{0:T(256)}, f32[3,33]{0,1:T(8,128)S(1)}, f32[768]{0:T(1024)}) all-reduce(f32[192]{0:T(256)S(1)} %reduce_sum.660, f32[192]{0:T(256)S(1)} %reduce_sum.665, f32[3,33]{0,1:T(8,128)S(1)} %pad_add_fusion.7, f32[768]{0:T(1024)S(1)} %copy-done.266), channel_id=1, replica_groups=mesh['dp'=8,'tensor'=4] {'dp'}, use_global_device_ids=true, to_apply=%region_39.40 | all-reduce | flops 1251 | bytes 10008 | tf_op jit(solution)/shard_map/psum | solution.py:244
  588.7 3.0 add_reduce_fusion
  591.8 41.7 %all-reduce.68 = (f32[768]{0:T(1024)}, f32[768]{0:T(1024)}, f32[768]{0:T(1024)}, f32[768]{0:T(1024)}, f32[768]{0:T(1024)}, /*index=5*/f32[768]{0:T(1024)}) all-reduce(f32[768]{0:T(1024)S(1)} %get-tuple-element.203, f32[768]{0:T(1024)S(1)} %copy-done.250, ...), channel_id=1, replica_groups=mesh['dp'=8,'tensor'=4] {'dp','tensor'}, use_global_device_ids=true, to_apply=%region_79.80 | all-reduce | flops 4608 | bytes 36864 | tf_op jit(solution)/shard_map/psum | solution.py:260
  633.4 166.4 %all-reduce.73.cloned.1.call-done = (f32[768,192]{0,1:T(8,128)}, f32[768,192]{0,1:T(8,128)}, f32[768,192]{0,1:T(8,128)}, f32[192,768]{1,0:T(8,128)}, f32[768,768]{1,0:T(8,128)}, /*index=5*/f32[768,768]{1,0:T(8,128)}) async-done(((f32[768,192]{0,1:T(8,128)}, f32[768,192]{0,1:T(8,128)}, f32[768,192]{0,1:T(8,128)}, f32[192,768]{1,0:T(8,128)}, f32[768,768]{1,0:T(8,128)}, /*index=5*/f32[768,768]{1,0:T(8,128)}), ...) | async-done | bytes 7077904 | tf_op jit(solution)/shard_map/psum | solution.py:244
  (831 shorter events, 119.4 us)
Async XLA Ops:
  7.2 169.5 %copy-start = (bf16[768,768]{1,0:T(8,128)(2,1)S(1)}, bf16[768,768]{1,0:T(8,128)(2,1)}, u32[]{:S(2)}) copy-start(bf16[768,768]{1,0:T(8,128)(2,1)} %param.31) | copy-start | bytes 3538948
  7.2 137.0 %reduce-scatter.5.cloned.1.call-start = ((), (), s32[]{:S(2)}) async-start(), calls=%async_computation.4 | async-start | bytes 7864320 | tf_op jit(solution)/shard_map/reduce_scatter | solution.py:149
  11.9 37.7 %copy-start.91 = (f32[64,64]{1,0:T(8,128)}, f32[64,64]{1,0:T(8,128)S(1)}, u32[]{:S(2)}) copy-start(f32[64,64]{1,0:T(8,128)S(1)} %fusion.149) | copy-start | bytes 49156
  11.9 37.3 %copy-start.39 = (f32[64,64]{1,0:T(8,128)}, f32[64,64]{1,0:T(8,128)S(1)}, u32[]{:S(2)}) copy-start(f32[64,64]{1,0:T(8,128)S(1)} %get-tuple-element.293) | copy-start | bytes 49156
  11.9 37.3 %copy-start.93 = (f32[64,64]{1,0:T(8,128)}, f32[64,64]{1,0:T(8,128)S(1)}, u32[]{:S(2)}) copy-start(f32[64,64]{1,0:T(8,128)S(1)} %get-tuple-element.294) | copy-start | bytes 49156
  24.6 12.4 %copy-start.235 = (s32[2,1024]{1,0:T(2,128)}, s32[2,1024]{1,0:T(2,128)S(1)}, u32[]{:S(2)}) copy-start(s32[2,1024]{1,0:T(2,128)S(1)} %eq.256) | copy-start | bytes 24580
  24.7 12.3 %copy-start.305 = (f32[2,64]{1,0:T(2,128)}, f32[2,64]{1,0:T(2,128)S(1)}, u32[]{:S(2)}) copy-start(f32[2,64]{1,0:T(2,128)S(1)} %convert_reduce_fusion.6) | copy-start | bytes 1540
  24.9 18.0 %copy-start.255 = (pred[64,64]{1,0:T(8,128)(4,1)}, pred[64,64]{1,0:T(8,128)(4,1)S(1)}, u32[]{:S(2)}) copy-start(pred[64,64]{1,0:T(8,128)(4,1)S(1)} %copy.157) | copy-start | bytes 12292
  28.9 7.0 copy-start.100
  53.6 6.6 copy-start.89
  60.9 17.2 %copy-start.126 = (f32[2,3,64,64]{3,2,1,0:T(8,128)}, f32[2,3,64,64]{3,2,1,0:T(8,128)S(1)}, u32[]{:S(2)}) copy-start(f32[2,3,64,64]{3,2,1,0:T(8,128)S(1)} %fusion.182) | copy-start | bytes 294916
  82.9 61.2 %copy-start.257 = (f32[768]{0:T(1024)S(1)}, f32[768]{0:T(1024)}, u32[]{:S(2)}) copy-start(f32[768]{0:T(1024)} %param.28) | copy-start | bytes 9220
  83.0 93.7 %all-gather.3.cloned.1.call-start = ((), (), s32[]{:S(2)}) async-start(), calls=%async_computation.5 | async-start | bytes 3932160 | tf_op jit(solution)/shard_map/all_gather | solution.py:157
  146.8 29.9 %copy-start.312 = (f32[768]{0:T(1024)S(1)}, f32[768]{0:T(1024)}, u32[]{:S(2)}) copy-start(f32[768]{0:T(1024)} %param.32) | copy-start | bytes 9220
  148.0 112.1 %reduce-scatter.7.cloned.1.call-start = ((), (), s32[]{:S(2)}) async-start(), calls=%async_computation.6 | async-start | bytes 7864320 | tf_op jit(solution)/shard_map/reduce_scatter | solution.py:161
  176.7 20.4 %copy-start.311 = (bf16[768,768]{1,0:T(8,128)(2,1)S(1)}, bf16[768,768]{1,0:T(8,128)(2,1)}, u32[]{:S(2)}) copy-start(bf16[768,768]{1,0:T(8,128)(2,1)} %param.33) | copy-start | bytes 3538948
  201.5 58.5 %copy-start.267 = (f32[768]{0:T(1024)S(1)}, f32[768]{0:T(1024)}, u32[]{:S(2)}) copy-start(f32[768]{0:T(1024)} %param.34) | copy-start | bytes 9220
  201.5 96.2 %all-gather.5.cloned.1.call-start = ((), (), s32[]{:S(2)}) async-start(), calls=%async_computation.7 | async-start | bytes 3932160 | tf_op jit(solution)/shard_map/all_gather | solution.py:170
  269.0 84.0 %reduce-scatter.9.cloned.1.call-start = ((), (), s32[]{:S(2)}) async-start(), calls=%async_computation.8 | async-start | bytes 3932160 | tf_op jit(solution)/shard_map/reduce_scatter | solution.py:176
  314.9 273.8 %reduce-scatter.11.cloned.1.call-start = ((), (), s32[]{:S(2)}) async-start(), calls=%async_computation.9 | async-start | bytes 3932160 | tf_op jit(solution)/shard_map/reduce_scatter | solution.py:227
  359.1 20.0 %copy-start.213 = (f32[2,3,64]{2,1,0:T(4,128)S(1)}, f32[2,3,64]{2,1,0:T(4,128)}, u32[]{:S(2)}) copy-start(f32[2,3,64]{2,1,0:T(4,128)} %copy-done.212) | copy-start | bytes 4612
  360.2 18.9 %collective-permute-start = (bf16[512,768]{1,0:T(8,128)(2,1)}, bf16[512,768]{1,0:T(8,128)(2,1)}, u32[]{:S(2)}, u32[]{:S(2)}) collective-permute-start(bf16[512,768]{1,0:T(8,128)(2,1)} %get-tuple-element.183), channel_id=1, source_target_pairs={{0,1},{1,2},{2,3},{3,0},{4,5},{5,6},{6,7},{7,4},{8,9},{9,10},{10,1... | collective-permute-start | bytes 2359304 | tf_op jit(solution)/shard_map/ppermute | solution.py:198
  360.8 23.5 %collective-permute-start.1 = (bf16[512,768]{1,0:T(8,128)(2,1)}, bf16[512,768]{1,0:T(8,128)(2,1)}, u32[]{:S(2)}, u32[]{:S(2)}) collective-permute-start(bf16[512,768]{1,0:T(8,128)(2,1)} %get-tuple-element.183), channel_id=1, source_target_pairs={{0,3},{1,0},{2,1},{3,2},{4,7},{5,4},{6,5},{7,6},{8,11},{9,8},{10,9... | collective-permute-start | bytes 2359304 | tf_op jit(solution)/shard_map/ppermute | solution.py:205
  379.1 11.7 %collective-permute-start.2 = (bf16[512,768]{1,0:T(8,128)(2,1)}, bf16[512,768]{1,0:T(8,128)(2,1)}, u32[]{:S(2)}, u32[]{:S(2)}) collective-permute-start(bf16[512,768]{1,0:T(8,128)(2,1)} %collective-permute-done), channel_id=1, source_target_pairs={{0,1},{1,2},{2,3},{3,0},{4,5},{5,6},{6,7},{7,4},{8,9},{9,10},{10,1... | collective-permute-start | bytes 2359304 | tf_op jit(solution)/shard_map/ppermute | solution.py:198
  384.2 7.8 copy-start.13
  384.2 7.8 copy-start.96
  401.5 47.6 %copy-start.109 = (f32[2,3,64,64]{3,2,1,0:T(8,128)}, f32[2,3,64,64]{3,2,1,0:T(8,128)S(1)}, u32[]{:S(2)}) copy-start(f32[2,3,64,64]{3,2,1,0:T(8,128)S(1)} %fusion.185) | copy-start | bytes 294916
  432.7 6.5 copy-start.135
  432.7 6.5 copy-start.138
  432.7 6.5 copy-start.141
  432.7 6.5 copy-start.144
  432.7 6.5 copy-start.153
  432.8 6.5 copy-start.156
  432.8 6.5 copy-start.159
  432.8 6.5 copy-start.162
  432.8 6.5 copy-start.165
  472.7 8.5 %copy-start.24 = (bf16[24,8,2,1024]{3,1,2,0:T(8,128)(2,1)}, bf16[24,8,2,1024]{3,1,2,0:T(8,128)(2,1)S(1)}, u32[]{:S(2)}) copy-start(bf16[24,8,2,1024]{3,1,2,0:T(8,128)(2,1)S(1)} %copy.273) | copy-start | bytes 2359300
  485.0 20.5 %copy-start.10 = (f32[2,3,64,1024]{3,2,1,0:T(8,128)S(1)}, f32[2,3,64,1024]{3,2,1,0:T(8,128)}, u32[]{:S(2)}) copy-start(f32[2,3,64,1024]{3,2,1,0:T(8,128)} %copy-done.8) | copy-start | bytes 4718596
  485.0 20.6 %copy-start.110 = (f32[2,3,64,64]{3,2,1,0:T(8,128)S(1)}, f32[2,3,64,64]{3,2,1,0:T(8,128)}, u32[]{:S(2)}) copy-start(f32[2,3,64,64]{3,2,1,0:T(8,128)} %copy-done.109) | copy-start | bytes 294916
  485.0 20.6 %copy-start.211 = (f32[2,3,64]{2,1,0:T(4,128)S(1)}, f32[2,3,64]{2,1,0:T(4,128)}, u32[]{:S(2)}) copy-start(f32[2,3,64]{2,1,0:T(4,128)} %copy-done.209) | copy-start | bytes 4612
  485.0 20.6 %copy-start.215 = (f32[2,3,64]{2,1,0:T(4,128)S(1)}, f32[2,3,64]{2,1,0:T(4,128)}, u32[]{:S(2)}) copy-start(f32[2,3,64]{2,1,0:T(4,128)} %copy-done.212) | copy-start | bytes 4612
  505.5 8.8 %slice-start = ((s8[6291456]{0:T(1024)(128)(4,1)}), s8[4194304]{0:T(1024)(128)(4,1)S(1)}, s32[]{:S(2)}) async-start(s8[6291456]{0:T(1024)(128)(4,1)} %bitcast.353), calls=%async_computation.11 | async-start | bytes 8388608
  505.6 8.8 %slice-start.1 = ((s8[6291456]{0:T(1024)(128)(4,1)}), s8[2097152]{0:T(1024)(128)(4,1)S(1)}, s32[]{:S(2)}) async-start(s8[6291456]{0:T(1024)(128)(4,1)} %bitcast.353), calls=%async_computation.12 | async-start | bytes 4194304
  505.6 8.8 %copy-start.4 = (f32[2048,768]{1,0:T(8,128)S(1)}, f32[2048,768]{1,0:T(8,128)}, u32[]{:S(2)}) copy-start(f32[2048,768]{1,0:T(8,128)} %fusion.199) | copy-start | bytes 18874372
  517.1 282.7 %all-reduce.73.cloned.1.call-start = ((), (), s32[]{:S(2)}) async-start(), calls=%async_computation.10 | async-start | bytes 14155776 | tf_op jit(solution)/shard_map/psum | solution.py:244
  517.2 7.1 copy-start.310
  517.2 7.1 copy-start.316
  545.4 43.3 %copy-start.238 = (f32[512]{0:T(512)S(1)}, f32[512]{0:T(512)}, u32[]{:S(2)}) copy-start(f32[512]{0:T(512)} %copy-done.237) | copy-start | bytes 6148
  (281 other events, 750.6 us)
Sparse Core Ops, SparseCore 0:
  83.1 61.0 reduce-scatter.4
  148.1 28.5 all-gather.2
  201.7 58.3 reduce-scatter.6
  269.1 28.5 all-gather.4
  315.0 37.9 reduce-scatter.8
  517.2 37.6 reduce-scatter.10
  561.2 238.5 all-reduce.72
